TPU v7x, 32 devices: a whole 2x2x4 slice. The times are simulated.
32 devices in a mesh: group: 2 (over x), mem: 16 (over z, y, core).
Axes of the slice: x: 2, y: 2, z: 4, core: 2. Of those that a mesh axis runs over, the one named last changes fastest.
Arguments:
- perturbations: bfloat16 [32, 256, 4, 1, 256], P(('group', 'mem')), parts along dimension 0, may hold values from -6 to 6
- gradient: bfloat16 [512, 4, 1, 256], P(('group', 'mem')), parts along dimension 0, may hold values from -6 to 6
Outputs:
- increment: bfloat16 [512, 4, 1, 256], P(('group', 'mem')), parts along dimension 0
There are 2 independent parts, one for each index of `group`. A program takes and returns all parts, laid end to end along the dimension named above; each array names one. Nothing has to cross between parts.
All inputs are finite; a program needn't handle non-finite values.
Results may differ from a plain program's by a relative error of at most 0.0085.
Values may be sent and summed in bfloat16 or wider, within the bound.
No kernel may reach another device: no remote copies, remote signals or barrier semaphores. Data moves between devices by JAX's collectives and lax.ppermute only.
A program may use at most 64 MiB of HBM per device.

v0:
```python
import functools

import jax
import jax.numpy as jnp
from jax import lax
from jax.experimental import pallas as pl
from jax.experimental.pallas import tpu as pltpu
from jax.sharding import PartitionSpec as P


REACH = 8
GRANT = 16 << 20


def make_band(order):
    rows = jnp.arange(order, dtype=jnp.int32)
    offset = (rows[:, None] - rows[None, :]).astype(jnp.float32)
    weights = jnp.exp(-(offset * offset) / (4.0 * REACH))
    inside = jnp.abs(offset) <= REACH
    return jnp.where(inside, weights, jnp.float32(0.0)).astype(jnp.bfloat16)


def by_rows(perturbations, gradient):
    local_rows, _, levels, columns = gradient.shape
    count_here = perturbations.shape[0]
    grid_rows = perturbations.shape[1]
    members = count_here * lax.axis_size("mem")
    band_x = make_band(columns)
    band_y = make_band(grid_rows)
    row_block = lax.all_to_all(perturbations, "mem", split_axis=1, concat_axis=0, tiled=True)
    mixed = jnp.sum(
        row_block.astype(jnp.float32) * gradient.astype(jnp.float32)[None], axis=2
    ).astype(jnp.bfloat16)
    along_x = jnp.dot(
        mixed.reshape(members * local_rows * levels, columns),
        band_x,
        preferred_element_type=jnp.float32,
    )
    along_x = along_x.astype(jnp.bfloat16).reshape(members, local_rows, levels, columns)
    whole_field = lax.all_to_all(along_x, "mem", split_axis=0, concat_axis=1, tiled=True)
    whole_field = whole_field.reshape(count_here, grid_rows, levels * columns)
    filtered = jnp.stack(
        [jnp.dot(band_y, field, preferred_element_type=jnp.float32) for field in whole_field]
    )
    filtered = filtered.astype(jnp.bfloat16).reshape(count_here, grid_rows, levels, columns)
    row_field = lax.all_to_all(filtered, "mem", split_axis=1, concat_axis=0, tiled=True)
    total = jnp.sum(
        row_block.astype(jnp.float32) * row_field.astype(jnp.float32)[:, :, None], axis=0
    )
    return (total * (1.0 / (members - 1))).astype(jnp.bfloat16)


HALF, PAIR, SIDE, CORE = 8, 4, 2, 1
PEERS = (PAIR + SIDE, SIDE, PAIR)


def swap(array, bits):
    return lax.ppermute(array, "mem", [(i, i ^ bits) for i in range(16)])


def edges(array):
    pairs = []
    for i in range(16):
        half, place, core = i // 8, i // 2 % 4, i % 2
        place = (place + (1 if core else 3)) % 4
        pairs.append((i, half * 8 + place * 2 + core))
    return lax.ppermute(array, "mem", pairs)


def first_row(strip, chip, rows):
    start = jnp.clip(chip * strip - REACH, 0, rows - strip - 2 * REACH)
    return start, chip * strip - start


def window_kernel(strip, wanted, member_ref, grad_ref, *refs):
    outs, sem = refs[:-1], refs[-1]
    me = lax.axis_index("mem")
    rows = member_ref.shape[0]
    copies = [pltpu.make_async_copy(grad_ref, outs[len(wanted)], sem.at[len(wanted)])]
    for k, bits in enumerate(wanted):
        start, _ = first_row(strip, (me ^ bits) // 2, rows)
        copies.append(pltpu.make_async_copy(member_ref.at[pl.ds(start, strip + 2 * REACH)], outs[k], sem.at[k]))
    for copy in copies:
        copy.start()
    for copy in copies:
        copy.wait()


def windows(member, grad, strip, wanted):
    shape = (strip + 2 * REACH,) + member.shape[1:]
    outs = [jax.ShapeDtypeStruct(shape, member.dtype)] * len(wanted) + [jax.ShapeDtypeStruct(grad.shape, grad.dtype)]
    return pl.pallas_call(
        functools.partial(window_kernel, strip, wanted),
        out_shape=outs,
        in_specs=[pl.BlockSpec(memory_space=pltpu.HBM)] * 2,
        out_specs=[pl.BlockSpec(memory_space=pltpu.VMEM)] * len(outs),
        scratch_shapes=[pltpu.SemaphoreType.DMA((len(outs),))],
        compiler_params=pltpu.CompilerParams(vmem_limit_bytes=GRANT),
        name="windows",
    )(member, grad)


def strip_kernel(rows, far, me_ref, a_ref, b_ref, c_ref, d_ref, block_ref, edge_ref, mate_ref, band_ref,
                 own_ref, other_ref, grad_ref, mixed_ref, total_ref):
    me = me_ref[0]
    core, place = me % 2, me // 2 % 4
    part, reach = block_ref.shape[0], edge_ref.shape[1]
    strip = 2 * part
    chips = rows // strip
    chip = (me ^ (HALF * far)) // 2
    _, at = first_row(strip, chip, rows)
    span = strip + 2 * reach

    grad_ref[...] = jnp.zeros_like(grad_ref)
    grad_ref[pl.ds(at + core * part, part)] = block_ref[...]
    grad_ref[pl.ds(at + (1 - core) * part, part)] = mate_ref[pl.ds(far * part, part)]
    before = jnp.where(place == 0, 1 - far, far)
    after = jnp.where(place == 3, 1 - far, far)

    @pl.when(jnp.logical_and(chip > 0, core == 0))
    def _():
        grad_ref[pl.ds(at - reach, reach)] = mate_ref[pl.ds(2 * part + before * reach, reach)]

    @pl.when(jnp.logical_and(chip > 0, core == 1))
    def _():
        grad_ref[pl.ds(at - reach, reach)] = edge_ref[before]

    @pl.when(jnp.logical_and(chip < chips - 1, core == 0))
    def _():
        grad_ref[pl.ds(at + strip, reach)] = edge_ref[after]

    @pl.when(jnp.logical_and(chip < chips - 1, core == 1))
    def _():
        grad_ref[pl.ds(at + strip, reach)] = mate_ref[pl.ds(2 * part + after * reach, reach)]

    grad = grad_ref[...].astype(jnp.float32)
    members = (a_ref, b_ref, c_ref, d_ref)
    nvars, columns = grad.shape[1:]
    grad = grad.reshape(span * nvars, columns)
    row = lax.broadcasted_iota(jnp.int32, (span, span * nvars), 1) // nvars
    pick = jnp.where(row == lax.broadcasted_iota(jnp.int32, row.shape, 0), 1.0, 0.0).astype(jnp.bfloat16)
    for k, ref in enumerate(members):
        terms = ref[...].reshape(span * nvars, columns).astype(jnp.float32) * grad
        high = terms.astype(jnp.bfloat16)
        low = (terms - high.astype(jnp.float32)).astype(jnp.bfloat16)
        mixed = jnp.dot(pick, high, preferred_element_type=jnp.float32)
        mixed = mixed + jnp.dot(pick, low, preferred_element_type=jnp.float32)
        mixed_ref[pl.ds(k * span, span)] = mixed.astype(jnp.bfloat16)
    along = jnp.dot(mixed_ref[...], band_ref[...], preferred_element_type=jnp.float32).astype(jnp.bfloat16)
    offset = lax.broadcasted_iota(jnp.int32, (strip, span), 0) + at - lax.broadcasted_iota(jnp.int32, (strip, span), 1)
    wide = offset.astype(jnp.float32)
    band = jnp.exp(-(wide * wide) / (4.0 * REACH))
    band = jnp.where(jnp.abs(wide) <= REACH, band, 0.0).astype(jnp.bfloat16)
    total = None
    for k, ref in enumerate(members):
        field = jnp.dot(band, along[k * span : (k + 1) * span], preferred_element_type=jnp.float32)
        field = field.astype(jnp.bfloat16).astype(jnp.float32)
        term = ref[pl.ds(at, strip)].astype(jnp.float32) * field[:, None, :]
        total = term if total is None else total + term
    total_ref[...] = total
    own_ref[...] = total_ref[pl.ds(core * part, part)].astype(own_ref.dtype)
    other_ref[...] = total_ref[pl.ds((1 - core) * part, part)].astype(other_ref.dtype)


def one_strip(me, members, block, edge, mate, band, rows, far):
    nvars, columns = block.shape[1:]
    part = block.shape[0]
    span = 2 * part + 2 * edge.shape[1]
    piece = (part, nvars, columns)
    vmem = pl.BlockSpec(memory_space=pltpu.VMEM)
    return pl.pallas_call(
        functools.partial(strip_kernel, rows, far),
        out_shape=[
            jax.ShapeDtypeStruct(piece, jnp.float32),
            jax.ShapeDtypeStruct(piece, jnp.bfloat16),
        ],
        in_specs=[pl.BlockSpec(memory_space=pltpu.SMEM)] + [vmem] * 8,
        out_specs=[vmem] * 2,
        scratch_shapes=[
            pltpu.VMEM((span, nvars, columns), jnp.bfloat16),
            pltpu.VMEM((4 * span, columns), jnp.bfloat16),
            pltpu.VMEM((2 * part, nvars, columns), jnp.float32),
        ],
        compiler_params=pltpu.CompilerParams(vmem_limit_bytes=GRANT),
        name="far" if far else "near",
    )(me, *members, block, edge, mate, band)


def by_halves(perturbations, gradient):
    local_rows, nvars, _, columns = gradient.shape
    grid_rows = perturbations.shape[1]
    strip = 2 * local_rows
    members = lax.axis_size("mem")
    at = lax.axis_index("mem")
    me = at.reshape(1).astype(jnp.int32)
    param = gradient.reshape(local_rows, nvars, columns)
    member = pltpu.with_memory_space_constraint(perturbations.reshape(-1, nvars, columns), pltpu.HBM)
    stays = pltpu.with_memory_space_constraint(param, pltpu.HBM)

    wanted = [p ^ HALF for p in PEERS] + list(PEERS) + [HALF, 0]
    there = swap(param, HALF)
    *out, far_mine, near_mine, here = windows(member, stays, strip, wanted)
    far_in = [far_mine] + [swap(block, p) for block, p in zip(out[:3], PEERS)]
    near_in = [near_mine] + [swap(block, p) for block, p in zip(out[3:], PEERS)]
    both = jnp.stack([here, there])
    both = jnp.where(at & 1 == 0, both[:, :REACH], both[:, -REACH:])
    edge = edges(both)
    early = swap(jnp.concatenate([here, there]), CORE)
    mate = jnp.concatenate([early, swap(jnp.concatenate([edge[0], edge[1]]), CORE)])

    band = make_band(columns)
    args = (edge, mate, band, grid_rows)
    far_own, far_other = one_strip(me, far_in, there, *args, 1)
    far_sum = far_own + swap(far_other, CORE).astype(jnp.float32)
    far_sum = swap(far_sum.astype(jnp.bfloat16), HALF).astype(jnp.float32)
    near_own, near_other = one_strip(me, near_in, here, *args, 0)
    near_other = swap(near_other, CORE)
    total = near_own + near_other.astype(jnp.float32) + far_sum
    return (total * (1.0 / (members - 1))).astype(jnp.bfloat16).reshape(gradient.shape)


def solution(mesh):
    in_specs = (P(("group", "mem"), None, None, None, None), P(("group", "mem"), None, None, None))
    out_specs = P(("group", "mem"), None, None, None)
    halves = mesh.shape["mem"] == 16

    def per_device(perturbations, gradient):
        count_here, grid_rows, _, levels, _ = perturbations.shape
        local_rows = gradient.shape[0]
        if not halves:
            return by_rows(perturbations, gradient)
        assert count_here == 1 and levels == 1 and local_rows % 8 == 0 and grid_rows == 16 * local_rows
        return by_halves(perturbations, gradient)

    return jax.shard_map(
        per_device, mesh=mesh, in_specs=in_specs, out_specs=out_specs, check_vma=False
    )
```

profile of v0, /device:TPU:0, one launch (start us, length us, event | category | flops | bytes accessed | tf_op | source)
XLA Modules:
  0.0 33.0 jit_solution(315390685412618595)
XLA Ops:
  0.0 4.1 %collective-permute-start.3 = (bf16[16,4,256]{2,1,0:T(4,128)(2,1)}, bf16[16,4,256]{2,1,0:T(4,128)(2,1)S(1)}, u32[]{:S(2)}, u32[]{:S(2)}) collective-permute-start(bf16[16,4,256]{2,1,0:T(4,128)(2,1)} %bitcast.16), channel_id=1, source_target_pairs={{0,8},{1,9},{2,10},{3,11},{4,12},{5,13},{6,14},{7,15},{8,0},{9,1},... | collective-permute-start | bytes 98312 | tf_op jit(solution)/shard_map/ppermute | solution.py:58
  4.1 1.3 %windows.1 = (bf16[48,4,256]{2,1,0:T(4,128)(2,1)S(1)}, bf16[48,4,256]{2,1,0:T(4,128)(2,1)S(1)}, bf16[48,4,256]{2,1,0:T(4,128)(2,1)S(1)}, bf16[48,4,256]{2,1,0:T(...) custom-call(bf16[256,4,256]{2,1,0:T(4,128)(2,1)} %bitcast.15, ...), custom_call_target="tpu_custom_call" | custom-call | tf_op jit(solution)/shard_map/windows/pallas_call | solution.py:92
  5.4 2.6 %collective-permute-start = (bf16[48,4,256]{2,1,0:T(4,128)(2,1)S(1)}, bf16[48,4,256]{2,1,0:T(4,128)(2,1)S(1)}, u32[]{:S(2)}, u32[]{:S(2)}) collective-permute-start(bf16[48,4,256]{2,1,0:T(4,128)(2,1)S(1)} %get-tuple-element.19), channel_id=1, source_target_pairs={{0,6},{1,7},{2,4},{3,5},{4,2},{5,3},{6,0},{7,1},{8,14},{9,15},{10,... | collective-permute-start | bytes 294920 | tf_op jit(solution)/shard_map/ppermute | solution.py:58
  8.0 0.5 %collective-permute-start.1 = (bf16[48,4,256]{2,1,0:T(4,128)(2,1)S(1)}, bf16[48,4,256]{2,1,0:T(4,128)(2,1)S(1)}, u32[]{:S(2)}, u32[]{:S(2)}) collective-permute-start(bf16[48,4,256]{2,1,0:T(4,128)(2,1)S(1)} %get-tuple-element.20), channel_id=1, source_target_pairs={{0,2},{1,3},{2,0},{3,1},{4,6},{5,7},{6,4},{7,5},{8,10},{9,11},{10,... | collective-permute-start | bytes 294920 | tf_op jit(solution)/shard_map/ppermute | solution.py:58
  8.5 0.4 %collective-permute-start.2 = (bf16[48,4,256]{2,1,0:T(4,128)(2,1)S(1)}, bf16[48,4,256]{2,1,0:T(4,128)(2,1)S(1)}, u32[]{:S(2)}, u32[]{:S(2)}) collective-permute-start(bf16[48,4,256]{2,1,0:T(4,128)(2,1)S(1)} %get-tuple-element.21), channel_id=1, source_target_pairs={{0,4},{1,5},{2,6},{3,7},{4,0},{5,1},{6,2},{7,3},{8,12},{9,13},{10,... | collective-permute-start | bytes 294920 | tf_op jit(solution)/shard_map/ppermute | solution.py:58
  8.9 1.6 %collective-permute-start.10 = (bf16[48,4,256]{2,1,0:T(4,128)(2,1)S(1)}, bf16[48,4,256]{2,1,0:T(4,128)(2,1)S(1)}, u32[]{:S(2)}, u32[]{:S(2)}) collective-permute-start(bf16[48,4,256]{2,1,0:T(4,128)(2,1)S(1)} %get-tuple-element.28), channel_id=1, source_target_pairs={{0,4},{1,5},{2,6},{3,7},{4,0},{5,1},{6,2},{7,3},{8,12},{9,13},{10,... | collective-permute-start | bytes 294920 | tf_op jit(solution)/shard_map/ppermute | solution.py:58
  10.5 0.1 select_convert_fusion.band_ref
  10.6 0.0 collective-permute-done.3.block_ref
  10.7 1.5 %collective-permute-start.4 = (bf16[2,8,4,256]{3,2,1,0:T(4,128)(2,1)S(1)}, bf16[2,8,4,256]{3,2,1,0:T(4,128)(2,1)S(1)}, u32[]{:S(2)}, u32[]{:S(2)}) collective-permute-start(bf16[2,8,4,256]{3,2,1,0:T(4,128)(2,1)S(1)} %fusion.2), channel_id=1, source_target_pairs={{0,6},{1,3},{2,0},{3,5},{4,2},{5,7},{6,4},{7,1},{8,14},{9,11},{10,... | collective-permute-start | bytes 98312 | tf_op jit(solution)/shard_map/ppermute | solution.py:67
  12.2 2.5 %collective-permute-done.4.edge_ref = bf16[2,8,4,256]{3,2,1,0:T(4,128)(2,1)S(1)} collective-permute-done((bf16[2,8,4,256]{3,2,1,0:T(4,128)(2,1)S(1)}, bf16[2,8,4,256]{3,2,1,0:T(4,128)(2,1)S(1)}, u32[]{:S(2)}, u32[]{:S(2)}) %collective-permute-start.4) | collective-permute-done | bytes 32800 | tf_op jit(solution)/shard_map/ppermute | solution.py:67
  14.7 1.2 %collective-permute-done.5 = bf16[32,4,256]{2,1,0:T(4,128)(2,1)S(1)} collective-permute-done((bf16[32,4,256]{2,1,0:T(4,128)(2,1)S(1)}, bf16[32,4,256]{2,1,0:T(4,128)(2,1)S(1)}, u32[]{:S(2)}, u32[]{:S(2)}) %collective-permute-start.5) | collective-permute-done | bytes 65568 | tf_op jit(solution)/shard_map/ppermute | solution.py:58
  15.9 0.2 collective-permute-start.6
  16.1 1.0 %collective-permute-done.6 = bf16[16,4,256]{2,1,0:T(4,128)(2,1)S(1)} collective-permute-done((bf16[16,4,256]{2,1,0:T(4,128)(2,1)S(1)}, bf16[16,4,256]{2,1,0:T(4,128)(2,1)S(1)}, u32[]{:S(2)}, u32[]{:S(2)}) %collective-permute-start.6) | collective-permute-done | bytes 32800 | tf_op jit(solution)/shard_map/ppermute | solution.py:58
  17.1 3.1 %collective-permute-start.8 = (bf16[48,4,256]{2,1,0:T(4,128)(2,1)S(1)}, bf16[48,4,256]{2,1,0:T(4,128)(2,1)S(1)}, u32[]{:S(2)}, u32[]{:S(2)}) collective-permute-start(bf16[48,4,256]{2,1,0:T(4,128)(2,1)S(1)} %get-tuple-element.26), channel_id=1, source_target_pairs={{0,6},{1,7},{2,4},{3,5},{4,2},{5,3},{6,0},{7,1},{8,14},{9,15},{10,... | collective-permute-start | bytes 294920 | tf_op jit(solution)/shard_map/ppermute | solution.py:58
  20.2 3.2 %collective-permute-done.8.b_ref = bf16[48,4,256]{2,1,0:T(4,128)(2,1)S(1)} collective-permute-done((bf16[48,4,256]{2,1,0:T(4,128)(2,1)S(1)}, bf16[48,4,256]{2,1,0:T(4,128)(2,1)S(1)}, u32[]{:S(2)}, u32[]{:S(2)}) %collective-permute-start.8) | collective-permute-done | bytes 98336 | tf_op jit(solution)/shard_map/ppermute | solution.py:58
  23.4 2.0 %collective-permute-done.9.c_ref = bf16[48,4,256]{2,1,0:T(4,128)(2,1)S(1)} collective-permute-done((bf16[48,4,256]{2,1,0:T(4,128)(2,1)S(1)}, bf16[48,4,256]{2,1,0:T(4,128)(2,1)S(1)}, u32[]{:S(2)}, u32[]{:S(2)}) %collective-permute-start.9) | collective-permute-done | bytes 98336 | tf_op jit(solution)/shard_map/ppermute | solution.py:58
  25.4 0.7 %far.1 = (f32[16,4,256]{2,1,0:T(4,128)S(1)}, bf16[16,4,256]{2,1,0:T(4,128)(2,1)S(1)}) custom-call(s32[1]{0:T(128)} %bitcast.me_ref, bf16[48,4,256]{2,1,0:T(4,128)(2,1)S(1)} %get-tuple-element.25.a_ref, bf16[48,4,256]{2,1,0:T(4,128)(2,1)S(1)} %collective-permute-done.8.b_ref, bf16[48,4,256]{2,1,0:T(4,128)(2,1)S(1)} %collective-permute-done.9.c_ref, ...), custom_call_target="tpu_custom_call" | custom-call | tf_op jit(solution)/shard_map/far/pallas_call | solution.py:171
  26.1 0.1 collective-permute-start.11
  26.2 0.7 %near.1 = (f32[16,4,256]{2,1,0:T(4,128)S(1)}, bf16[16,4,256]{2,1,0:T(4,128)(2,1)S(1)}) custom-call(s32[1]{0:T(128)} %bitcast.me_ref, bf16[48,4,256]{2,1,0:T(4,128)(2,1)S(1)} %get-tuple-element.18.a_ref, bf16[48,4,256]{2,1,0:T(4,128)(2,1)S(1)} %collective-permute-done.b_ref, bf16[48,4,256]{2,1,0:T(4,128)(2,1)S(1)} %collective-permute-done.1.c_ref, ...), custom_call_target="tpu_custom_call" | custom-call | tf_op jit(solution)/shard_map/near/pallas_call | solution.py:171
  26.9 0.5 %collective-permute-start.7 = (bf16[16,4,256]{2,1,0:T(4,128)(2,1)S(1)}, bf16[16,4,256]{2,1,0:T(4,128)(2,1)S(1)}, u32[]{:S(2)}, u32[]{:S(2)}) collective-permute-start(bf16[16,4,256]{2,1,0:T(4,128)(2,1)S(1)} %get-tuple-element.24), channel_id=1, source_target_pairs={{0,1},{1,0},{2,3},{3,2},{4,5},{5,4},{6,7},{7,6},{8,9},{9,8},{10,11... | collective-permute-start | bytes 98312 | tf_op jit(solution)/shard_map/ppermute | solution.py:58
  27.5 0.7 %collective-permute-start.12 = (bf16[16,4,256]{2,1,0:T(4,128)(2,1)S(1)}, bf16[16,4,256]{2,1,0:T(4,128)(2,1)S(1)}, u32[]{:S(2)}, u32[]{:S(2)}) collective-permute-start(bf16[16,4,256]{2,1,0:T(4,128)(2,1)S(1)} %add_convert_fusion), channel_id=1, source_target_pairs={{0,8},{1,9},{2,10},{3,11},{4,12},{5,13},{6,14},{7,15},{8,0},{9,1},... | collective-permute-start | bytes 98312 | tf_op jit(solution)/shard_map/ppermute | solution.py:58
  28.2 0.1 collective-permute-done.7
  28.4 4.0 %collective-permute-done.12 = bf16[16,4,256]{2,1,0:T(4,128)(2,1)S(1)} collective-permute-done((bf16[16,4,256]{2,1,0:T(4,128)(2,1)S(1)}, bf16[16,4,256]{2,1,0:T(4,128)(2,1)S(1)}, u32[]{:S(2)}, u32[]{:S(2)}) %collective-permute-start.12) | collective-permute-done | bytes 32800 | tf_op jit(solution)/shard_map/ppermute | solution.py:58
  32.4 0.6 %fusion = bf16[16,4,1,256]{3,1,2,0:T(4,128)(2,1)} fusion(bf16[16,4,256]{2,1,0:T(4,128)(2,1)S(1)} %collective-permute-done.12, f32[16,4,256]{2,1,0:T(4,128)S(1)} %get-tuple-element.23, bf16[16,4,256]{2,1,0:T(4,128)(2,1)S(1)} %collective-permute-done.7), kind=kLoop, calls=%fused_computation.7 | loop fusion | flops 98304 | bytes 163840 | tf_op jit(solution)/shard_map/reshape | solution.py:219
  (14 shorter events, 0.2 us)
Async XLA Ops:
  0.0 10.6 %collective-permute-start.3 = (bf16[16,4,256]{2,1,0:T(4,128)(2,1)}, bf16[16,4,256]{2,1,0:T(4,128)(2,1)S(1)}, u32[]{:S(2)}, u32[]{:S(2)}) collective-permute-start(bf16[16,4,256]{2,1,0:T(4,128)(2,1)} %bitcast.16), channel_id=1, source_target_pairs={{0,8},{1,9},{2,10},{3,11},{4,12},{5,13},{6,14},{7,15},{8,0},{9,1},... | collective-permute-start | bytes 98312 | tf_op jit(solution)/shard_map/ppermute | solution.py:58
  5.4 20.8 %collective-permute-start = (bf16[48,4,256]{2,1,0:T(4,128)(2,1)S(1)}, bf16[48,4,256]{2,1,0:T(4,128)(2,1)S(1)}, u32[]{:S(2)}, u32[]{:S(2)}) collective-permute-start(bf16[48,4,256]{2,1,0:T(4,128)(2,1)S(1)} %get-tuple-element.19), channel_id=1, source_target_pairs={{0,6},{1,7},{2,4},{3,5},{4,2},{5,3},{6,0},{7,1},{8,14},{9,15},{10,... | collective-permute-start | bytes 294920 | tf_op jit(solution)/shard_map/ppermute | solution.py:58
  8.0 18.3 %collective-permute-start.1 = (bf16[48,4,256]{2,1,0:T(4,128)(2,1)S(1)}, bf16[48,4,256]{2,1,0:T(4,128)(2,1)S(1)}, u32[]{:S(2)}, u32[]{:S(2)}) collective-permute-start(bf16[48,4,256]{2,1,0:T(4,128)(2,1)S(1)} %get-tuple-element.20), channel_id=1, source_target_pairs={{0,2},{1,3},{2,0},{3,1},{4,6},{5,7},{6,4},{7,5},{8,10},{9,11},{10,... | collective-permute-start | bytes 294920 | tf_op jit(solution)/shard_map/ppermute | solution.py:58
  8.5 17.8 %collective-permute-start.2 = (bf16[48,4,256]{2,1,0:T(4,128)(2,1)S(1)}, bf16[48,4,256]{2,1,0:T(4,128)(2,1)S(1)}, u32[]{:S(2)}, u32[]{:S(2)}) collective-permute-start(bf16[48,4,256]{2,1,0:T(4,128)(2,1)S(1)} %get-tuple-element.21), channel_id=1, source_target_pairs={{0,4},{1,5},{2,6},{3,7},{4,0},{5,1},{6,2},{7,3},{8,12},{9,13},{10,... | collective-permute-start | bytes 294920 | tf_op jit(solution)/shard_map/ppermute | solution.py:58
  8.9 11.3 %collective-permute-start.10 = (bf16[48,4,256]{2,1,0:T(4,128)(2,1)S(1)}, bf16[48,4,256]{2,1,0:T(4,128)(2,1)S(1)}, u32[]{:S(2)}, u32[]{:S(2)}) collective-permute-start(bf16[48,4,256]{2,1,0:T(4,128)(2,1)S(1)} %get-tuple-element.28), channel_id=1, source_target_pairs={{0,4},{1,5},{2,6},{3,7},{4,0},{5,1},{6,2},{7,3},{8,12},{9,13},{10,... | collective-permute-start | bytes 294920 | tf_op jit(solution)/shard_map/ppermute | solution.py:58
  10.7 4.0 %collective-permute-start.4 = (bf16[2,8,4,256]{3,2,1,0:T(4,128)(2,1)S(1)}, bf16[2,8,4,256]{3,2,1,0:T(4,128)(2,1)S(1)}, u32[]{:S(2)}, u32[]{:S(2)}) collective-permute-start(bf16[2,8,4,256]{3,2,1,0:T(4,128)(2,1)S(1)} %fusion.2), channel_id=1, source_target_pairs={{0,6},{1,3},{2,0},{3,5},{4,2},{5,7},{6,4},{7,1},{8,14},{9,11},{10,... | collective-permute-start | bytes 98312 | tf_op jit(solution)/shard_map/ppermute | solution.py:67
  14.6 1.3 %collective-permute-start.5 = (bf16[32,4,256]{2,1,0:T(4,128)(2,1)S(1)}, bf16[32,4,256]{2,1,0:T(4,128)(2,1)S(1)}, u32[]{:S(2)}, u32[]{:S(2)}) collective-permute-start(bf16[32,4,256]{2,1,0:T(4,128)(2,1)S(1)} %pad_maximum_fusion), channel_id=1, source_target_pairs={{0,1},{1,0},{2,3},{3,2},{4,5},{5,4},{6,7},{7,6},{8,9},{9,8},{10,11... | collective-permute-start | bytes 196616 | tf_op jit(solution)/shard_map/ppermute | solution.py:58
  15.9 1.2 %collective-permute-start.6 = (bf16[16,4,256]{2,1,0:T(4,128)(2,1)S(1)}, bf16[16,4,256]{2,1,0:T(4,128)(2,1)S(1)}, u32[]{:S(2)}, u32[]{:S(2)}) collective-permute-start(bf16[16,4,256]{2,1,0:T(4,128)(2,1)S(1)} %pad_maximum_fusion.2), channel_id=1, source_target_pairs={{0,1},{1,0},{2,3},{3,2},{4,5},{5,4},{6,7},{7,6},{8,9},{9,8},{10,11... | collective-permute-start | bytes 98312 | tf_op jit(solution)/shard_map/ppermute | solution.py:58
  17.1 6.3 %collective-permute-start.8 = (bf16[48,4,256]{2,1,0:T(4,128)(2,1)S(1)}, bf16[48,4,256]{2,1,0:T(4,128)(2,1)S(1)}, u32[]{:S(2)}, u32[]{:S(2)}) collective-permute-start(bf16[48,4,256]{2,1,0:T(4,128)(2,1)S(1)} %get-tuple-element.26), channel_id=1, source_target_pairs={{0,6},{1,7},{2,4},{3,5},{4,2},{5,3},{6,0},{7,1},{8,14},{9,15},{10,... | collective-permute-start | bytes 294920 | tf_op jit(solution)/shard_map/ppermute | solution.py:58
  20.2 5.2 %collective-permute-start.9 = (bf16[48,4,256]{2,1,0:T(4,128)(2,1)S(1)}, bf16[48,4,256]{2,1,0:T(4,128)(2,1)S(1)}, u32[]{:S(2)}, u32[]{:S(2)}) collective-permute-start(bf16[48,4,256]{2,1,0:T(4,128)(2,1)S(1)} %get-tuple-element.27), channel_id=1, source_target_pairs={{0,2},{1,3},{2,0},{3,1},{4,6},{5,7},{6,4},{7,5},{8,10},{9,11},{10,... | collective-permute-start | bytes 294920 | tf_op jit(solution)/shard_map/ppermute | solution.py:58
  26.1 1.4 %collective-permute-start.11 = (bf16[16,4,256]{2,1,0:T(4,128)(2,1)S(1)}, bf16[16,4,256]{2,1,0:T(4,128)(2,1)S(1)}, u32[]{:S(2)}, u32[]{:S(2)}) collective-permute-start(bf16[16,4,256]{2,1,0:T(4,128)(2,1)S(1)} %get-tuple-element.30), channel_id=1, source_target_pairs={{0,1},{1,0},{2,3},{3,2},{4,5},{5,4},{6,7},{7,6},{8,9},{9,8},{10,11... | collective-permute-start | bytes 98312 | tf_op jit(solution)/shard_map/ppermute | solution.py:58
  26.9 1.4 %collective-permute-start.7 = (bf16[16,4,256]{2,1,0:T(4,128)(2,1)S(1)}, bf16[16,4,256]{2,1,0:T(4,128)(2,1)S(1)}, u32[]{:S(2)}, u32[]{:S(2)}) collective-permute-start(bf16[16,4,256]{2,1,0:T(4,128)(2,1)S(1)} %get-tuple-element.24), channel_id=1, source_target_pairs={{0,1},{1,0},{2,3},{3,2},{4,5},{5,4},{6,7},{7,6},{8,9},{9,8},{10,11... | collective-permute-start | bytes 98312 | tf_op jit(solution)/shard_map/ppermute | solution.py:58
  27.5 4.9 %collective-permute-start.12 = (bf16[16,4,256]{2,1,0:T(4,128)(2,1)S(1)}, bf16[16,4,256]{2,1,0:T(4,128)(2,1)S(1)}, u32[]{:S(2)}, u32[]{:S(2)}) collective-permute-start(bf16[16,4,256]{2,1,0:T(4,128)(2,1)S(1)} %add_convert_fusion), channel_id=1, source_target_pairs={{0,8},{1,9},{2,10},{3,11},{4,12},{5,13},{6,14},{7,15},{8,0},{9,1},... | collective-permute-start | bytes 98312 | tf_op jit(solution)/shard_map/ppermute | solution.py:58
where the time goes:
time: 33.2 us; the launch traced here: 33 us
  starting transfers between devices  15.2 us (46%)
  waiting for transfers between devices  14.1 us (42%)
  Pallas kernels  2.69 us (8%)
  other arithmetic  0.89 us (3%)
    ppermute x12, starting transfers between devices, swap(): return lax.ppermute(array, 'mem', [(i, i ^ bits) for i in range(16)])  13.8 us
    ppermute x12, waiting for transfers between devices, swap(): return lax.ppermute(array, 'mem', [(i, i ^ bits) for i in range(16)])  11.6 us
    ppermute x1, waiting for transfers between devices, edges(): return lax.ppermute(array, 'mem', pairs)  2.46 us
    ppermute x1, starting transfers between devices, edges(): return lax.ppermute(array, 'mem', pairs)  1.46 us
    pallas_call x2, Pallas kernels, one_strip(): pl.pallas_call(functools.partial(strip_kernel, rows, far), out_shape=[jax...  1.41 us
    pallas_call x1, Pallas kernels, windows(): pl.pallas_call(functools.partial(window_kernel, strip, wanted), out_shape...  1.28 us
  transfers between devices with their start and end apart: 13, of which 7 were waited for; matrix products, arithmetic and copies ran while one was open for 1% of the time, Pallas kernels for 8%

commit v1 on v0

--- a/solution.py
+++ b/solution.py
@@ -2,6 +2,7 @@
 
 import jax
 import jax.numpy as jnp
+import numpy as np
 from jax import lax
 from jax.experimental import pallas as pl
 from jax.experimental.pallas import tpu as pltpu
@@ -18,6 +19,12 @@
     weights = jnp.exp(-(offset * offset) / (4.0 * REACH))
     inside = jnp.abs(offset) <= REACH
     return jnp.where(inside, weights, jnp.float32(0.0)).astype(jnp.bfloat16)
+
+
+def fixed_band(order):
+    offset = np.arange(order)[:, None] - np.arange(order)[None, :]
+    weights = np.exp(-(offset.astype(np.float32) ** 2) / np.float32(4.0 * REACH))
+    return np.where(np.abs(offset) <= REACH, weights, np.float32(0.0)).astype(jnp.bfloat16)
 
 
 def by_rows(perturbations, gradient):
@@ -208,7 +215,7 @@
     early = swap(jnp.concatenate([here, there]), CORE)
     mate = jnp.concatenate([early, swap(jnp.concatenate([edge[0], edge[1]]), CORE)])
 
-    band = make_band(columns)
+    band = jnp.asarray(fixed_band(columns))
     args = (edge, mate, band, grid_rows)
     far_own, far_other = one_strip(me, far_in, there, *args, 1)
     far_sum = far_own + swap(far_other, CORE).astype(jnp.float32)

time: 33.2 us -> 32 us (0.964)
  starting transfers between devices: 15.2 us -> 14.1 us
    ppermute x1, waiting for transfers between devices: 2.46 us -> 3.93 us  [edges(): return lax.ppermute(array, 'mem', pairs)]
    ppermute x12, waiting for transfers between devices: 11.6 us -> 10.2 us  [swap(): return lax.ppermute(array, 'mem', [(i, i ^ bits) for i in range(16)])]
    ppermute x1, starting transfers between devices: 1.46 us -> 0.45 us  [edges(): return lax.ppermute(array, 'mem', pairs)]
where the time goes in v1:
time: 32 us; the launch traced here: 31.9 us
  starting transfers between devices  14.1 us (44%)
  waiting for transfers between devices  14.1 us (44%)
  Pallas kernels  2.7 us (8%)
  other arithmetic  0.79 us (2%)
    ppermute x12, starting transfers between devices, swap(): return lax.ppermute(array, 'mem', [(i, i ^ bits) for i in range(16)])  13.7 us
    ppermute x12, waiting for transfers between devices, swap(): return lax.ppermute(array, 'mem', [(i, i ^ bits) for i in range(16)])  10.2 us
    ppermute x1, waiting for transfers between devices, edges(): return lax.ppermute(array, 'mem', pairs)  3.93 us
    pallas_call x2, Pallas kernels, one_strip(): pl.pallas_call(functools.partial(strip_kernel, rows, far), out_shape=[jax...  1.41 us
    pallas_call x1, Pallas kernels, windows(): pl.pallas_call(functools.partial(window_kernel, strip, wanted), out_shape...  1.28 us
    reshape x1, other arithmetic, by_halves(): (total * (1.0 / (members - 1))).astype(jnp.bfloat16).reshape(gradient.shape)  0.65 us
  transfers between devices with their start and end apart: 13, of which 7 were waited for; matrix products, arithmetic and copies ran while one was open for 1% of the time, Pallas kernels for 8%

profile of v1, /device:TPU:0, one launch (start us, length us, event | category | flops | bytes accessed | tf_op | source)
XLA Modules:
  0.0 31.9 jit_solution(8326822470771522140)
XLA Ops:
  0.0 4.1 %collective-permute-start.3 = (bf16[16,4,256]{2,1,0:T(4,128)(2,1)}, bf16[16,4,256]{2,1,0:T(4,128)(2,1)S(1)}, u32[]{:S(2)}, u32[]{:S(2)}) collective-permute-start(bf16[16,4,256]{2,1,0:T(4,128)(2,1)} %bitcast.16), channel_id=1, source_target_pairs={{0,8},{1,9},{2,10},{3,11},{4,12},{5,13},{6,14},{7,15},{8,0},{9,1},... | collective-permute-start | bytes 98312 | tf_op jit(solution)/shard_map/ppermute | solution.py:65
  4.1 1.3 %windows.1 = (bf16[48,4,256]{2,1,0:T(4,128)(2,1)S(1)}, bf16[48,4,256]{2,1,0:T(4,128)(2,1)S(1)}, bf16[48,4,256]{2,1,0:T(4,128)(2,1)S(1)}, bf16[48,4,256]{2,1,0:T(...) custom-call(bf16[256,4,256]{2,1,0:T(4,128)(2,1)} %bitcast.15, ...), custom_call_target="tpu_custom_call" | custom-call | tf_op jit(solution)/shard_map/windows/pallas_call | solution.py:99
  5.4 2.6 %collective-permute-start = (bf16[48,4,256]{2,1,0:T(4,128)(2,1)S(1)}, bf16[48,4,256]{2,1,0:T(4,128)(2,1)S(1)}, u32[]{:S(2)}, u32[]{:S(2)}) collective-permute-start(bf16[48,4,256]{2,1,0:T(4,128)(2,1)S(1)} %get-tuple-element.19), channel_id=1, source_target_pairs={{0,6},{1,7},{2,4},{3,5},{4,2},{5,3},{6,0},{7,1},{8,14},{9,15},{10,... | collective-permute-start | bytes 294920 | tf_op jit(solution)/shard_map/ppermute | solution.py:65
  8.0 0.5 %collective-permute-start.1 = (bf16[48,4,256]{2,1,0:T(4,128)(2,1)S(1)}, bf16[48,4,256]{2,1,0:T(4,128)(2,1)S(1)}, u32[]{:S(2)}, u32[]{:S(2)}) collective-permute-start(bf16[48,4,256]{2,1,0:T(4,128)(2,1)S(1)} %get-tuple-element.20), channel_id=1, source_target_pairs={{0,2},{1,3},{2,0},{3,1},{4,6},{5,7},{6,4},{7,5},{8,10},{9,11},{10,... | collective-permute-start | bytes 294920 | tf_op jit(solution)/shard_map/ppermute | solution.py:65
  8.5 0.4 %collective-permute-start.2 = (bf16[48,4,256]{2,1,0:T(4,128)(2,1)S(1)}, bf16[48,4,256]{2,1,0:T(4,128)(2,1)S(1)}, u32[]{:S(2)}, u32[]{:S(2)}) collective-permute-start(bf16[48,4,256]{2,1,0:T(4,128)(2,1)S(1)} %get-tuple-element.21), channel_id=1, source_target_pairs={{0,4},{1,5},{2,6},{3,7},{4,0},{5,1},{6,2},{7,3},{8,12},{9,13},{10,... | collective-permute-start | bytes 294920 | tf_op jit(solution)/shard_map/ppermute | solution.py:65
  8.9 2.5 %collective-permute-start.8 = (bf16[48,4,256]{2,1,0:T(4,128)(2,1)S(1)}, bf16[48,4,256]{2,1,0:T(4,128)(2,1)S(1)}, u32[]{:S(2)}, u32[]{:S(2)}) collective-permute-start(bf16[48,4,256]{2,1,0:T(4,128)(2,1)S(1)} %get-tuple-element.26), channel_id=1, source_target_pairs={{0,6},{1,7},{2,4},{3,5},{4,2},{5,3},{6,0},{7,1},{8,14},{9,15},{10,... | collective-permute-start | bytes 294920 | tf_op jit(solution)/shard_map/ppermute | solution.py:65
  11.5 0.4 %collective-permute-start.4 = (bf16[2,8,4,256]{3,2,1,0:T(4,128)(2,1)S(1)}, bf16[2,8,4,256]{3,2,1,0:T(4,128)(2,1)S(1)}, u32[]{:S(2)}, u32[]{:S(2)}) collective-permute-start(bf16[2,8,4,256]{3,2,1,0:T(4,128)(2,1)S(1)} %fusion.2), channel_id=1, source_target_pairs={{0,6},{1,3},{2,0},{3,5},{4,2},{5,7},{6,4},{7,1},{8,14},{9,11},{10,... | collective-permute-start | bytes 98312 | tf_op jit(solution)/shard_map/ppermute | solution.py:74
  12.0 3.9 %collective-permute-done.4.edge_ref = bf16[2,8,4,256]{3,2,1,0:T(4,128)(2,1)S(1)} collective-permute-done((bf16[2,8,4,256]{3,2,1,0:T(4,128)(2,1)S(1)}, bf16[2,8,4,256]{3,2,1,0:T(4,128)(2,1)S(1)}, u32[]{:S(2)}, u32[]{:S(2)}) %collective-permute-start.4) | collective-permute-done | bytes 32800 | tf_op jit(solution)/shard_map/ppermute | solution.py:74
  15.9 0.0 copy-start
  16.0 1.2 %collective-permute-done.5 = bf16[32,4,256]{2,1,0:T(4,128)(2,1)S(1)} collective-permute-done((bf16[32,4,256]{2,1,0:T(4,128)(2,1)S(1)}, bf16[32,4,256]{2,1,0:T(4,128)(2,1)S(1)}, u32[]{:S(2)}, u32[]{:S(2)}) %collective-permute-start.5) | collective-permute-done | bytes 65568 | tf_op jit(solution)/shard_map/ppermute | solution.py:65
  17.2 0.2 collective-permute-start.6
  17.4 1.0 %collective-permute-done.6 = bf16[16,4,256]{2,1,0:T(4,128)(2,1)S(1)} collective-permute-done((bf16[16,4,256]{2,1,0:T(4,128)(2,1)S(1)}, bf16[16,4,256]{2,1,0:T(4,128)(2,1)S(1)}, u32[]{:S(2)}, u32[]{:S(2)}) %collective-permute-start.6) | collective-permute-done | bytes 32800 | tf_op jit(solution)/shard_map/ppermute | solution.py:65
  18.4 1.1 %collective-permute-start.9 = (bf16[48,4,256]{2,1,0:T(4,128)(2,1)S(1)}, bf16[48,4,256]{2,1,0:T(4,128)(2,1)S(1)}, u32[]{:S(2)}, u32[]{:S(2)}) collective-permute-start(bf16[48,4,256]{2,1,0:T(4,128)(2,1)S(1)} %get-tuple-element.27), channel_id=1, source_target_pairs={{0,2},{1,3},{2,0},{3,1},{4,6},{5,7},{6,4},{7,5},{8,10},{9,11},{10,... | collective-permute-start | bytes 294920 | tf_op jit(solution)/shard_map/ppermute | solution.py:65
  19.5 1.3 %collective-permute-start.10 = (bf16[48,4,256]{2,1,0:T(4,128)(2,1)S(1)}, bf16[48,4,256]{2,1,0:T(4,128)(2,1)S(1)}, u32[]{:S(2)}, u32[]{:S(2)}) collective-permute-start(bf16[48,4,256]{2,1,0:T(4,128)(2,1)S(1)} %get-tuple-element.28), channel_id=1, source_target_pairs={{0,4},{1,5},{2,6},{3,7},{4,0},{5,1},{6,2},{7,3},{8,12},{9,13},{10,... | collective-permute-start | bytes 294920 | tf_op jit(solution)/shard_map/ppermute | solution.py:65
  20.8 2.5 %collective-permute-done.9.c_ref = bf16[48,4,256]{2,1,0:T(4,128)(2,1)S(1)} collective-permute-done((bf16[48,4,256]{2,1,0:T(4,128)(2,1)S(1)}, bf16[48,4,256]{2,1,0:T(4,128)(2,1)S(1)}, u32[]{:S(2)}, u32[]{:S(2)}) %collective-permute-start.9) | collective-permute-done | bytes 98336 | tf_op jit(solution)/shard_map/ppermute | solution.py:65
  23.3 0.9 %collective-permute-done.10.d_ref = bf16[48,4,256]{2,1,0:T(4,128)(2,1)S(1)} collective-permute-done((bf16[48,4,256]{2,1,0:T(4,128)(2,1)S(1)}, bf16[48,4,256]{2,1,0:T(4,128)(2,1)S(1)}, u32[]{:S(2)}, u32[]{:S(2)}) %collective-permute-start.10) | collective-permute-done | bytes 98336 | tf_op jit(solution)/shard_map/ppermute | solution.py:65
  24.1 0.7 %far.1 = (f32[16,4,256]{2,1,0:T(4,128)S(1)}, bf16[16,4,256]{2,1,0:T(4,128)(2,1)S(1)}) custom-call(s32[1]{0:T(128)} %bitcast.me_ref, bf16[48,4,256]{2,1,0:T(4,128)(2,1)S(1)} %get-tuple-element.25.a_ref, bf16[48,4,256]{2,1,0:T(4,128)(2,1)S(1)} %collective-permute-done.8.b_ref, bf16[48,4,256]{2,1,0:T(4,128)(2,1)S(1)} %collective-permute-done.9.c_ref, ...), custom_call_target="tpu_custom_call" | custom-call | tf_op jit(solution)/shard_map/far/pallas_call | solution.py:178
  24.8 0.1 collective-permute-start.11
  24.9 0.7 %near.1 = (f32[16,4,256]{2,1,0:T(4,128)S(1)}, bf16[16,4,256]{2,1,0:T(4,128)(2,1)S(1)}) custom-call(s32[1]{0:T(128)} %bitcast.me_ref, bf16[48,4,256]{2,1,0:T(4,128)(2,1)S(1)} %get-tuple-element.18.a_ref, bf16[48,4,256]{2,1,0:T(4,128)(2,1)S(1)} %collective-permute-done.b_ref, bf16[48,4,256]{2,1,0:T(4,128)(2,1)S(1)} %collective-permute-done.1.c_ref, ...), custom_call_target="tpu_custom_call" | custom-call | tf_op jit(solution)/shard_map/near/pallas_call | solution.py:178
  25.7 0.5 %collective-permute-start.7 = (bf16[16,4,256]{2,1,0:T(4,128)(2,1)S(1)}, bf16[16,4,256]{2,1,0:T(4,128)(2,1)S(1)}, u32[]{:S(2)}, u32[]{:S(2)}) collective-permute-start(bf16[16,4,256]{2,1,0:T(4,128)(2,1)S(1)} %get-tuple-element.24), channel_id=1, source_target_pairs={{0,1},{1,0},{2,3},{3,2},{4,5},{5,4},{6,7},{7,6},{8,9},{9,8},{10,11... | collective-permute-start | bytes 98312 | tf_op jit(solution)/shard_map/ppermute | solution.py:65
  26.2 0.4 %collective-permute-start.12 = (bf16[16,4,256]{2,1,0:T(4,128)(2,1)S(1)}, bf16[16,4,256]{2,1,0:T(4,128)(2,1)S(1)}, u32[]{:S(2)}, u32[]{:S(2)}) collective-permute-start(bf16[16,4,256]{2,1,0:T(4,128)(2,1)S(1)} %add_convert_fusion), channel_id=1, source_target_pairs={{0,8},{1,9},{2,10},{3,11},{4,12},{5,13},{6,14},{7,15},{8,0},{9,1},... | collective-permute-start | bytes 98312 | tf_op jit(solution)/shard_map/ppermute | solution.py:65
  26.6 0.4 %collective-permute-done.7 = bf16[16,4,256]{2,1,0:T(4,128)(2,1)S(1)} collective-permute-done((bf16[16,4,256]{2,1,0:T(4,128)(2,1)S(1)}, bf16[16,4,256]{2,1,0:T(4,128)(2,1)S(1)}, u32[]{:S(2)}, u32[]{:S(2)}) %collective-permute-start.7) | collective-permute-done | bytes 32800 | tf_op jit(solution)/shard_map/ppermute | solution.py:65
  27.1 4.2 %collective-permute-done.12 = bf16[16,4,256]{2,1,0:T(4,128)(2,1)S(1)} collective-permute-done((bf16[16,4,256]{2,1,0:T(4,128)(2,1)S(1)}, bf16[16,4,256]{2,1,0:T(4,128)(2,1)S(1)}, u32[]{:S(2)}, u32[]{:S(2)}) %collective-permute-start.12) | collective-permute-done | bytes 32800 | tf_op jit(solution)/shard_map/ppermute | solution.py:65
  31.2 0.6 %fusion = bf16[16,4,1,256]{3,1,2,0:T(4,128)(2,1)} fusion(bf16[16,4,256]{2,1,0:T(4,128)(2,1)S(1)} %collective-permute-done.12, f32[16,4,256]{2,1,0:T(4,128)S(1)} %get-tuple-element.23, bf16[16,4,256]{2,1,0:T(4,128)(2,1)S(1)} %collective-permute-done.7), kind=kLoop, calls=%fused_computation.5 | loop fusion | flops 98304 | bytes 163840 | tf_op jit(solution)/shard_map/reshape | solution.py:226
  (15 shorter events, 0.2 us)
Async XLA Ops:
  0.0 11.4 %collective-permute-start.3 = (bf16[16,4,256]{2,1,0:T(4,128)(2,1)}, bf16[16,4,256]{2,1,0:T(4,128)(2,1)S(1)}, u32[]{:S(2)}, u32[]{:S(2)}) collective-permute-start(bf16[16,4,256]{2,1,0:T(4,128)(2,1)} %bitcast.16), channel_id=1, source_target_pairs={{0,8},{1,9},{2,10},{3,11},{4,12},{5,13},{6,14},{7,15},{8,0},{9,1},... | collective-permute-start | bytes 98312 | tf_op jit(solution)/shard_map/ppermute | solution.py:65
  5.4 19.5 %collective-permute-start = (bf16[48,4,256]{2,1,0:T(4,128)(2,1)S(1)}, bf16[48,4,256]{2,1,0:T(4,128)(2,1)S(1)}, u32[]{:S(2)}, u32[]{:S(2)}) collective-permute-start(bf16[48,4,256]{2,1,0:T(4,128)(2,1)S(1)} %get-tuple-element.19), channel_id=1, source_target_pairs={{0,6},{1,7},{2,4},{3,5},{4,2},{5,3},{6,0},{7,1},{8,14},{9,15},{10,... | collective-permute-start | bytes 294920 | tf_op jit(solution)/shard_map/ppermute | solution.py:65
  8.0 17.0 %collective-permute-start.1 = (bf16[48,4,256]{2,1,0:T(4,128)(2,1)S(1)}, bf16[48,4,256]{2,1,0:T(4,128)(2,1)S(1)}, u32[]{:S(2)}, u32[]{:S(2)}) collective-permute-start(bf16[48,4,256]{2,1,0:T(4,128)(2,1)S(1)} %get-tuple-element.20), channel_id=1, source_target_pairs={{0,2},{1,3},{2,0},{3,1},{4,6},{5,7},{6,4},{7,5},{8,10},{9,11},{10,... | collective-permute-start | bytes 294920 | tf_op jit(solution)/shard_map/ppermute | solution.py:65
  8.5 16.5 %collective-permute-start.2 = (bf16[48,4,256]{2,1,0:T(4,128)(2,1)S(1)}, bf16[48,4,256]{2,1,0:T(4,128)(2,1)S(1)}, u32[]{:S(2)}, u32[]{:S(2)}) collective-permute-start(bf16[48,4,256]{2,1,0:T(4,128)(2,1)S(1)} %get-tuple-element.21), channel_id=1, source_target_pairs={{0,4},{1,5},{2,6},{3,7},{4,0},{5,1},{6,2},{7,3},{8,12},{9,13},{10,... | collective-permute-start | bytes 294920 | tf_op jit(solution)/shard_map/ppermute | solution.py:65
  8.9 10.6 %collective-permute-start.8 = (bf16[48,4,256]{2,1,0:T(4,128)(2,1)S(1)}, bf16[48,4,256]{2,1,0:T(4,128)(2,1)S(1)}, u32[]{:S(2)}, u32[]{:S(2)}) collective-permute-start(bf16[48,4,256]{2,1,0:T(4,128)(2,1)S(1)} %get-tuple-element.26), channel_id=1, source_target_pairs={{0,6},{1,7},{2,4},{3,5},{4,2},{5,3},{6,0},{7,1},{8,14},{9,15},{10,... | collective-permute-start | bytes 294920 | tf_op jit(solution)/shard_map/ppermute | solution.py:65
  11.5 4.4 %collective-permute-start.4 = (bf16[2,8,4,256]{3,2,1,0:T(4,128)(2,1)S(1)}, bf16[2,8,4,256]{3,2,1,0:T(4,128)(2,1)S(1)}, u32[]{:S(2)}, u32[]{:S(2)}) collective-permute-start(bf16[2,8,4,256]{3,2,1,0:T(4,128)(2,1)S(1)} %fusion.2), channel_id=1, source_target_pairs={{0,6},{1,3},{2,0},{3,5},{4,2},{5,7},{6,4},{7,1},{8,14},{9,11},{10,... | collective-permute-start | bytes 98312 | tf_op jit(solution)/shard_map/ppermute | solution.py:74
  15.9 1.3 %collective-permute-start.5 = (bf16[32,4,256]{2,1,0:T(4,128)(2,1)S(1)}, bf16[32,4,256]{2,1,0:T(4,128)(2,1)S(1)}, u32[]{:S(2)}, u32[]{:S(2)}) collective-permute-start(bf16[32,4,256]{2,1,0:T(4,128)(2,1)S(1)} %pad_maximum_fusion), channel_id=1, source_target_pairs={{0,1},{1,0},{2,3},{3,2},{4,5},{5,4},{6,7},{7,6},{8,9},{9,8},{10,11... | collective-permute-start | bytes 196616 | tf_op jit(solution)/shard_map/ppermute | solution.py:65
  15.9 8.2 %copy-start = (bf16[256,256]{1,0:T(8,128)(2,1)S(1)}, bf16[256,256]{1,0:T(8,128)(2,1)}, u32[]{:S(2)}) copy-start(bf16[256,256]{1,0:T(8,128)(2,1)} %constant.12.clone.band_ref) | copy-start | bytes 393220
  17.2 1.2 %collective-permute-start.6 = (bf16[16,4,256]{2,1,0:T(4,128)(2,1)S(1)}, bf16[16,4,256]{2,1,0:T(4,128)(2,1)S(1)}, u32[]{:S(2)}, u32[]{:S(2)}) collective-permute-start(bf16[16,4,256]{2,1,0:T(4,128)(2,1)S(1)} %pad_maximum_fusion.2), channel_id=1, source_target_pairs={{0,1},{1,0},{2,3},{3,2},{4,5},{5,4},{6,7},{7,6},{8,9},{9,8},{10,11... | collective-permute-start | bytes 98312 | tf_op jit(solution)/shard_map/ppermute | solution.py:65
  18.4 4.9 %collective-permute-start.9 = (bf16[48,4,256]{2,1,0:T(4,128)(2,1)S(1)}, bf16[48,4,256]{2,1,0:T(4,128)(2,1)S(1)}, u32[]{:S(2)}, u32[]{:S(2)}) collective-permute-start(bf16[48,4,256]{2,1,0:T(4,128)(2,1)S(1)} %get-tuple-element.27), channel_id=1, source_target_pairs={{0,2},{1,3},{2,0},{3,1},{4,6},{5,7},{6,4},{7,5},{8,10},{9,11},{10,... | collective-permute-start | bytes 294920 | tf_op jit(solution)/shard_map/ppermute | solution.py:65
  19.5 4.6 %collective-permute-start.10 = (bf16[48,4,256]{2,1,0:T(4,128)(2,1)S(1)}, bf16[48,4,256]{2,1,0:T(4,128)(2,1)S(1)}, u32[]{:S(2)}, u32[]{:S(2)}) collective-permute-start(bf16[48,4,256]{2,1,0:T(4,128)(2,1)S(1)} %get-tuple-element.28), channel_id=1, source_target_pairs={{0,4},{1,5},{2,6},{3,7},{4,0},{5,1},{6,2},{7,3},{8,12},{9,13},{10,... | collective-permute-start | bytes 294920 | tf_op jit(solution)/shard_map/ppermute | solution.py:65
  24.8 1.4 %collective-permute-start.11 = (bf16[16,4,256]{2,1,0:T(4,128)(2,1)S(1)}, bf16[16,4,256]{2,1,0:T(4,128)(2,1)S(1)}, u32[]{:S(2)}, u32[]{:S(2)}) collective-permute-start(bf16[16,4,256]{2,1,0:T(4,128)(2,1)S(1)} %get-tuple-element.30), channel_id=1, source_target_pairs={{0,1},{1,0},{2,3},{3,2},{4,5},{5,4},{6,7},{7,6},{8,9},{9,8},{10,11... | collective-permute-start | bytes 98312 | tf_op jit(solution)/shard_map/ppermute | solution.py:65
  25.7 1.4 %collective-permute-start.7 = (bf16[16,4,256]{2,1,0:T(4,128)(2,1)S(1)}, bf16[16,4,256]{2,1,0:T(4,128)(2,1)S(1)}, u32[]{:S(2)}, u32[]{:S(2)}) collective-permute-start(bf16[16,4,256]{2,1,0:T(4,128)(2,1)S(1)} %get-tuple-element.24), channel_id=1, source_target_pairs={{0,1},{1,0},{2,3},{3,2},{4,5},{5,4},{6,7},{7,6},{8,9},{9,8},{10,11... | collective-permute-start | bytes 98312 | tf_op jit(solution)/shard_map/ppermute | solution.py:65
  26.2 5.0 %collective-permute-start.12 = (bf16[16,4,256]{2,1,0:T(4,128)(2,1)S(1)}, bf16[16,4,256]{2,1,0:T(4,128)(2,1)S(1)}, u32[]{:S(2)}, u32[]{:S(2)}) collective-permute-start(bf16[16,4,256]{2,1,0:T(4,128)(2,1)S(1)} %add_convert_fusion), channel_id=1, source_target_pairs={{0,8},{1,9},{2,10},{3,11},{4,12},{5,13},{6,14},{7,15},{8,0},{9,1},... | collective-permute-start | bytes 98312 | tf_op jit(solution)/shard_map/ppermute | solution.py:65
